TPU v7x, 128 devices: a whole 4x4x4 slice. The times are simulated.
128 devices in a mesh: dx: 8 (over y_lo, x), dy: 16 (over y_hi, z, core).
Axes of the slice: x: 4, y: 4 (y_hi: 2, y_lo: 2; y = y_hi * 2 + y_lo), z: 4, core: 2. Of those that a mesh axis runs over, the one named last changes fastest.
Arguments:
- fine_nodes: bfloat16 [256, 256, 512], P('dx', 'dy'), may hold values from -6 to 6
- fine_edges: bfloat16 [6, 256, 256, 512], P(None, 'dx', 'dy'), may hold values from -6 to 6
- fine_links: int32 [6, 256, 256], P(None, 'dx', 'dy'), may hold values from 0 to 48
- mid_nodes: bfloat16 [64, 64, 512], P('dx', 'dy'), may hold values from -6 to 6
- mid_edges: bfloat16 [6, 64, 64, 512], P(None, 'dx', 'dy'), may hold values from -6 to 6
- mid_links: int32 [6, 64, 64], P(None, 'dx', 'dy'), may hold values from 0 to 8
- coarse_nodes: bfloat16 [16, 16, 512], replicated, may hold values from -6 to 6
- coarse_edges: bfloat16 [6, 16, 16, 512], replicated, may hold values from -6 to 6
- coarse_links: int32 [6, 16, 16], replicated, may hold values from 0 to 255
- edge_self: bfloat16 [1, 512, 1536], replicated, may hold values from -0.25 to 0.25
- edge_sender: bfloat16 [1, 512, 1536], replicated, may hold values from -0.25 to 0.25
- edge_receiver: bfloat16 [1, 512, 1536], replicated, may hold values from -0.25 to 0.25
- edge_bias: float32 [1, 1536], replicated, may hold values from -6 to 6
- edge_output: bfloat16 [1, 1536, 512], replicated, may hold values from -0.15625 to 0.15625
- edge_gain: float32 [1, 512], replicated, may hold values from 0.1 to 1.9
- edge_shift: float32 [1, 512], replicated, may hold values from -3 to 3
- node_self: bfloat16 [1, 512, 1536], replicated, may hold values from -0.25 to 0.25
- node_summed: bfloat16 [1, 512, 1536], replicated, may hold values from -0.109375 to 0.109375
- node_bias: float32 [1, 1536], replicated, may hold values from -6 to 6
- node_output: bfloat16 [1, 1536, 512], replicated, may hold values from -0.15625 to 0.15625
- node_gain: float32 [1, 512], replicated, may hold values from 0.1 to 1.9
- node_shift: float32 [1, 512], replicated, may hold values from -3 to 3
- prolongation: bfloat16 [1, 512, 512], replicated, may hold values from -0.25 to 0.25
- pooling: bfloat16 [1, 512, 512], replicated, may hold values from -0.25 to 0.25
Outputs:
- fine_out: bfloat16 [256, 256, 512], P('dx', 'dy')
- fine_edges_out: bfloat16 [6, 256, 256, 512], P(None, 'dx', 'dy')
- mid_out: bfloat16 [64, 64, 512], P('dx', 'dy')
- mid_edges_out: bfloat16 [6, 64, 64, 512], P(None, 'dx', 'dy')
- coarse_out: bfloat16 [16, 16, 512], replicated
- coarse_edges_out: bfloat16 [6, 16, 16, 512], replicated
Inputs may be any that keep to these rules, and one draw needn't show every extreme that they name: `fine_links`: code q names the sender at offset (q // 7 - 3, q % 7 - 3) from the receiver. `mid_links`: code q names the sender at offset (q // 3 - 1, q % 3 - 1) from the receiver.
All inputs are finite; a program needn't handle non-finite values.
Results may differ from a plain program's by a relative error of at most 0.012.
Values may be sent and summed in bfloat16 or wider, within the bound.
No kernel may reach another device: no remote copies, remote signals or barrier semaphores. Data moves between devices by JAX's collectives and lax.ppermute only.
A program may use at most 128 MiB of HBM per device.

v0:
```python
import jax
import jax.numpy as jnp
from jax import lax
from jax.sharding import Mesh
from jax.sharding import PartitionSpec as P

FINE_REACH = 3
MID_REACH = 1
DX = ("dx_0", "dx_1")
DY = ("dy_0", "dy_1", "dy_2")
epsilon = 1e-05


def with_halo(value, sides, width):
    for axis, dim in sides:
        count, length = (lax.axis_size(axis), value.shape[dim])
        up = [(i, (i + 1) % count) for i in range(count)]
        down = [(j, i) for i, j in up]
        last = lax.slice_in_dim(value, length - width, length, axis=dim)
        leading = lax.slice_in_dim(value, 0, width, axis=dim)
        before = lax.ppermute(last, axis, up)
        after = lax.ppermute(leading, axis, down)
        value = jnp.concatenate([before, value, after], axis=dim)
    return value


def joined_along(blocks, dim):
    dims = list(blocks.shape[1:])
    dims[dim] *= blocks.shape[0]
    return jnp.moveaxis(blocks, 0, dim).reshape(dims)


def all_blocks(value, axes, turns):
    blocks = value[None]
    for k in turns:
        blocks = lax.all_gather(blocks, axes[k], axis=0, tiled=True)
    block = [lax.axis_size(axes[k]) for k in reversed(turns)]
    blocks = blocks.reshape(*block, *value.shape)
    turned = sorted(range(len(turns)), key=lambda place: turns[len(turns) - 1 - place])
    return blocks.transpose(*turned, *range(len(turns), blocks.ndim)).reshape(-1, *value.shape)


def gather_axes(value, axes, turns, dim):
    return joined_along(all_blocks(value, axes, turns), dim)


def normalize(values, gain_term, shift_term):
    average = jnp.mean(values, axis=-1, keepdims=True)
    centred = values - average
    variance = jnp.mean(centred * centred, axis=-1, keepdims=True)
    return centred * lax.rsqrt(variance + epsilon) * gain_term + shift_term


def level_update(nodes, edges, sender_terms, senders, weights):
    (
        self_matrix,
        receiver_matrix,
        edge_bias,
        edge_output,
        edge_gain,
        edge_shift,
        node_self,
        node_summed,
        node_bias,
        node_output,
        node_gain,
        node_shift,
    ) = weights
    fanout, height, breadth, feature = edges.shape
    places = height * breadth
    flat_nodes = nodes.reshape(places, feature)
    flat_edges = edges.reshape(fanout * places, feature)
    receiver = jnp.dot(flat_nodes, receiver_matrix, preferred_element_type=jnp.float32) + edge_bias
    latent = jnp.dot(flat_edges, self_matrix, preferred_element_type=jnp.float32).reshape(
        fanout, places, -1
    )
    latent = (
        latent + jnp.take(sender_terms, senders.reshape(fanout, places), axis=0) + receiver[None]
    )
    hidden = jax.nn.silu(latent).astype(jnp.bfloat16).reshape(fanout * places, -1)
    message = jnp.dot(hidden, edge_output, preferred_element_type=jnp.float32)
    new_edges = (flat_edges.astype(jnp.float32) + normalize(message, edge_gain, edge_shift)).astype(
        jnp.bfloat16
    )
    new_edges = new_edges.reshape(fanout, places, feature)
    summed = jnp.sum(new_edges.astype(jnp.float32), axis=0).astype(jnp.bfloat16)
    node_hidden = jnp.dot(flat_nodes, node_self, preferred_element_type=jnp.float32)
    node_hidden = (
        node_hidden + jnp.dot(summed, node_summed, preferred_element_type=jnp.float32) + node_bias
    )
    node_hidden = jax.nn.silu(node_hidden).astype(jnp.bfloat16)
    node_message = jnp.dot(node_hidden, node_output, preferred_element_type=jnp.float32)
    new_nodes = (
        flat_nodes.astype(jnp.float32) + normalize(node_message, node_gain, node_shift)
    ).astype(jnp.bfloat16)
    return (
        new_nodes.reshape(height, breadth, feature),
        new_edges.reshape(fanout, height, breadth, feature),
    )


def offset_index(link_codes, reach_cells, padded_breadth):
    window_span = 2 * reach_cells + 1
    row_place = lax.broadcasted_iota(jnp.int32, link_codes.shape, 1)
    col_place = lax.broadcasted_iota(jnp.int32, link_codes.shape, 2)
    return (
        (row_place + link_codes // window_span) * padded_breadth
        + col_place
        + link_codes % window_span
    )


def widen(parent_values, height, breadth):
    parent_rows, parent_cols, feature = parent_values.shape
    spread_out = jnp.broadcast_to(
        parent_values[:, None, :, None, :], (parent_rows, 4, parent_cols, 4, feature)
    )
    return spread_out.reshape(height, breadth, feature)


def assemble_nodes(pieces, across, along):
    total, block_rows, block_cols, feature = pieces.shape
    arranged = pieces.reshape(across, along, block_rows, block_cols, feature).transpose(
        0, 2, 1, 3, 4
    )
    return arranged.reshape(across * block_rows, along * block_cols, feature)


def per_device(
    fine_nodes,
    fine_edges,
    fine_links,
    mid_nodes,
    mid_edges,
    mid_links,
    coarse_nodes,
    coarse_edges,
    coarse_links,
    edge_self,
    edge_sender,
    edge_receiver,
    edge_bias,
    edge_output,
    edge_gain,
    edge_shift,
    node_self,
    node_summed,
    node_bias,
    node_output,
    node_gain,
    node_shift,
    prolongation,
    pooling,
):
    tile_rows, tile_cols, feature = fine_nodes.shape
    mid_rows, mid_cols = (tile_rows // 4, tile_cols // 4)
    block_rows, block_cols = (tile_rows // 16, tile_cols // 16)
    coarse_rows, coarse_cols = (coarse_nodes.shape[0], coarse_nodes.shape[1])
    across = lax.axis_size(DX)
    along = lax.axis_size(DY)
    first_index = lax.axis_index(DX)
    second_index = lax.axis_index(DY)
    row_offset = first_index * block_rows
    col_offset = second_index * block_cols
    zero_offset = jnp.zeros((), jnp.int32)
    weights = tuple(
        (
            stacked[0]
            for stacked in (
                edge_self,
                edge_receiver,
                edge_bias,
                edge_output,
                edge_gain,
                edge_shift,
                node_self,
                node_summed,
                node_bias,
                node_output,
                node_gain,
                node_shift,
            )
        )
    )
    sender_matrix = edge_sender[0]
    fine_rim = with_halo(fine_nodes, ((DX, 0), (DY, 1)), FINE_REACH)
    fine_terms = jnp.dot(
        fine_rim.reshape(-1, feature), sender_matrix, preferred_element_type=jnp.float32
    )
    fine_index = offset_index(fine_links, FINE_REACH, tile_cols + 2 * FINE_REACH)
    fine_new, fine_edges = level_update(fine_nodes, fine_edges, fine_terms, fine_index, weights)
    pooled = (
        mid_nodes.astype(jnp.float32)
        .reshape(block_rows, 4, block_cols, 4, feature)
        .mean(axis=(1, 3))
        .astype(jnp.bfloat16)
    )
    raised = jnp.dot(pooled.reshape(-1, feature), pooling[0], preferred_element_type=jnp.float32)
    own_coarse = lax.dynamic_slice(
        coarse_nodes, (row_offset, col_offset, zero_offset), (block_rows, block_cols, feature)
    )
    own_coarse = (
        own_coarse.astype(jnp.float32) + raised.reshape(block_rows, block_cols, feature)
    ).astype(jnp.bfloat16)
    gathered = gather_axes(own_coarse[None], (("dx_0", "dx_1", "dy_0", "dy_1"), "dy_2"), (0, 1), 0)
    coarse_nodes = assemble_nodes(gathered, across, along)
    coarse_terms = jnp.dot(
        coarse_nodes.reshape(-1, feature), sender_matrix, preferred_element_type=jnp.float32
    )
    coarse_nodes, coarse_edges = level_update(
        coarse_nodes, coarse_edges, coarse_terms, coarse_links, weights
    )
    lifted = jnp.dot(
        coarse_nodes.reshape(-1, feature), prolongation[0], preferred_element_type=jnp.float32
    )
    lifted = lifted.reshape(coarse_rows, coarse_cols, feature)
    mid_source = mid_nodes
    mid_rim = with_halo(mid_source, ((DX, 0), (DY, 1)), MID_REACH)
    row_places = (
        first_index * mid_rows - MID_REACH + jnp.arange(mid_rows + 2 * MID_REACH, dtype=jnp.int32)
    )
    col_places = (
        second_index * mid_cols - MID_REACH + jnp.arange(mid_cols + 2 * MID_REACH, dtype=jnp.int32)
    )
    row_parent = row_places % (coarse_rows * 4) // 4
    col_parent = col_places % (coarse_cols * 4) // 4
    rim_lift = jnp.take(jnp.take(lifted, row_parent, axis=0), col_parent, axis=1)
    mid_rim = (mid_rim.astype(jnp.float32) + rim_lift).astype(jnp.bfloat16)
    mid_nodes = mid_rim[MID_REACH : MID_REACH + mid_rows, MID_REACH : MID_REACH + mid_cols]
    mid_terms = jnp.dot(
        mid_rim.reshape(-1, feature), sender_matrix, preferred_element_type=jnp.float32
    )
    mid_index = offset_index(mid_links, MID_REACH, mid_cols + 2 * MID_REACH)
    mid_nodes, mid_edges = level_update(mid_nodes, mid_edges, mid_terms, mid_index, weights)
    lifted_mid = jnp.dot(
        mid_nodes.reshape(-1, feature), prolongation[0], preferred_element_type=jnp.float32
    )
    lifted_mid = lifted_mid.reshape(mid_rows, mid_cols, feature)
    fine_nodes = (fine_new.astype(jnp.float32) + widen(lifted_mid, tile_rows, tile_cols)).astype(
        jnp.bfloat16
    )
    return (fine_nodes, fine_edges, mid_nodes, mid_edges, coarse_nodes, coarse_edges)


def solution(mesh):
    torus = Mesh(mesh.devices.reshape(2, 4, 2, 4, 2), ("dx_0", "dx_1", "dy_0", "dy_1", "dy_2"))
    in_specs = (
        P(DX, DY, None),
        P(None, DX, DY, None),
        P(None, DX, DY),
        P(DX, DY, None),
        P(None, DX, DY, None),
        P(None, DX, DY),
        P(),
        P(),
        P(),
        P(),
        P(),
        P(),
        P(),
        P(),
        P(),
        P(),
        P(),
        P(),
        P(),
        P(),
        P(),
        P(),
        P(),
        P(),
    )
    out_specs = (
        P(DX, DY, None),
        P(None, DX, DY, None),
        P(DX, DY, None),
        P(None, DX, DY, None),
        P(),
        P(),
    )
    return jax.shard_map(
        per_device, mesh=torus, in_specs=in_specs, out_specs=out_specs, check_vma=False
    )
```

profile of v0, /device:TPU:0, one launch (start us, length us, event | category | flops | bytes accessed | tf_op | source)
XLA Modules:
  0.0 355.0 jit_solution(18027557386560085851)
XLA Ops:
  0.6 1.6 fusion.84
  2.2 1.6 collective-permute-start
  3.8 2.5 collective-permute-start.1
  7.8 4.1 %collective-permute-start.5 = (bf16[1,4,512]{2,0,1:T(2,128)(2,1)}, bf16[1,4,512]{2,0,1:T(2,128)(2,1)}, u32[]{:S(2)}, u32[]{:S(2)}) collective-permute-start(bf16[1,4,512]{2,0,1:T(2,128)(2,1)} %get-tuple-element.13), channel_id=1, source_target_pairs={{16,0},{32,16},{48,32},{64,48},{80,64},{96,80},{112,96},{0,112},{1... | collective-permute-start | bytes 12296 | tf_op jit(solution)/shard_map/ppermute | solution.py:22
  20.0 176.0 %all-gather = bf16[128,1,512]{2,1,0:T(2,128)(2,1)S(1)} all-gather(bf16[2,1,512]{2,1,0:T(2,128)(2,1)S(1)} %copy.119), channel_id=2, replica_groups=mesh['dx_0'=2,'dx_1'=4,'dy_0'=2,'dy_1'=4,'dy_2'=2] {'dx_0','dx_1','dy_0'..., dimensions={0}, use_global_device_ids=true | all-gather | bytes 133120 | tf_op jit(solution)/shard_map/all_gather | solution.py:36
  196.9 2.2 all_gather.7
  199.5 3.9 %fusion.37 = f32[512,1536]{1,0:T(8,128)} fusion(bf16[512,512]{1,0:T(8,128)(2,1)} %bitcast.175, bf16[1,512,1536]{2,1,0:T(8,128)(2,1)S(1)} %copy-done.1), kind=kOutput, calls=%fused_computation.56 | convolution fusion | flops 805306368 | bytes 5242880 | tf_op jit(solution)/shard_map/dot_general | solution.py:87
  203.4 2.6 convolution_add_fusion.1
  206.0 1.7 convolution_add_fusion.3
  207.7 1.7 fusion.35
  211.1 2.0 fusion.26
  213.2 6.7 %gather_fusion.1 = f32[1536,1536]{1,0:T(8,128)} fusion(f32[256,1536]{1,0:T(8,128)S(1)} %fusion.26, s32[2048]{0:T(1024)S(1)} %pad_clamp_fusion), kind=kCustom, calls=%fused_computation.1 | custom fusion | bytes 18880512 | tf_op jit(solution)/shard_map/jit(_take)/gather | solution.py:78
  219.9 7.3 %multiply_convert_fusion.1 = bf16[6,256,1536]{2,1,0:T(8,128)(2,1)S(1)} fusion(f32[6,256,1536]{2,1,0:T(8,128)} %bitcast.169, bf16[6,256,512]{2,1,0:T(8,128)(2,1)} %bitcast.180, f32[256,1536]{1,0:T(8,128)} %convolution_add_fusion.3, pred[6,256]{1,0:T(8,128)(4,1)S(1)} %compare_and_fusion.1, bf16[1,512,1536]{2,1,0:T(8,128)(2,1)S(1)} %copy-done), kind=kOutput, calls=%fused_computation.6 | convolution fusion | flops 2434793472 | bytes 18875904 | tf_op jit(solution)/shard_map/dot_general | solution.py:74
  227.2 2.7 fusion.86
  233.6 4.4 %fusion.87 = (f32[256]{0:T(256)S(1)}, f32[256,512]{1,0:T(8,128)}) fusion(bf16[1,1536,512]{2,1,0:T(8,128)(2,1)} %param.43, f32[256,1536]{1,0:T(8,128)} %fusion.35, bf16[256,512]{1,0:T(8,128)(2,1)} %reduce_sum.170, bf16[1,512,1536]{2,1,0:T(8,128)(2,1)} %param.41, f32[1536]{0:T(1024)S(1)} %reduce.7), kind=kOutput, calls=%fused_computation.187 | convolution fusion | flops 808189696 | bytes 5512192 | tf_op jit(solution)/shard_map/dot_general | solution.py:92
  244.8 5.2 %collective-permute-start.7 = (bf16[10,1,512]{2,0,1:T(8,128)(2,1)}, bf16[10,1,512]{2,0,1:T(8,128)(2,1)}, u32[]{:S(2)}, u32[]{:S(2)}) collective-permute-start(bf16[10,1,512]{2,0,1:T(8,128)(2,1)} %get-tuple-element.11), channel_id=1, source_target_pairs={{1,0},{2,1},{3,2},{4,3},{5,4},{6,5},{7,6},{8,7},{9,8},{10,9},{11,1... | collective-permute-start | bytes 30728 | tf_op jit(solution)/shard_map/ppermute | solution.py:22
  252.4 2.5 gather_fusion.3
  258.7 2.5 convolution_add_fusion.6
  263.1 1.8 fusion.24
  266.0 1.7 multiply_convert_fusion.4
  268.9 2.7 fusion.91
  275.3 5.4 %collective-permute-start.3 = (bf16[38,3,512]{2,1,0:T(4,128)(2,1)}, bf16[38,3,512]{2,1,0:T(4,128)(2,1)S(1)}, u32[]{:S(2)}, u32[]{:S(2)}) collective-permute-start(bf16[38,3,512]{2,1,0:T(4,128)(2,1)} %get-tuple-element.7), channel_id=1, source_target_pairs={{1,0},{2,1},{3,2},{4,3},{5,4},{6,5},{7,6},{8,7},{9,8},{10,9},{11,1... | collective-permute-start | bytes 350216 | tf_op jit(solution)/shard_map/ppermute | solution.py:22
  283.8 2.6 pad_maximum_fusion
  286.3 2.1 reshape.524
  288.5 5.0 %fusion.28 = f32[836,1536]{1,0:T(8,128)} fusion(bf16[836,512]{1,0:T(8,128)(2,1)} %reshape.524, bf16[1,512,1536]{2,1,0:T(8,128)(2,1)S(1)} %copy-done.4), kind=kOutput, calls=%fused_computation.47 | convolution fusion | flops 1314914304 | bytes 7565312 | tf_op jit(solution)/shard_map/dot_general | solution.py:187
  293.5 23.1 %gather_fusion = f32[3072,1536]{1,0:T(8,128)} fusion(f32[836,1536]{1,0:T(8,128)} %fusion.28, s32[3072]{0:T(1024)S(1)} %copy-done.26), kind=kCustom, calls=%fused_computation | custom fusion | bytes 37761024 | tf_op jit(solution)/shard_map/jit(_take)/gather | solution.py:78
  316.6 14.7 %multiply_convert_fusion = bf16[6,512,1536]{2,1,0:T(8,128)(2,1)} fusion(f32[6,512,1536]{2,1,0:T(8,128)} %bitcast.166, f32[512,1536]{1,0:T(8,128)} %convolution_add_fusion.1, pred[6,512]{1,0:T(8,128)(4,1)S(1)} %copy-done.43, bf16[6,512,512]{2,1,0:T(8,128)(2,1)} %bitcast.177, bf16[1,512,1536]{2,1,0:T(8,128)(2,1)S(1)} %copy-done), kind=kOutput, calls=%fused_computation.5 | convolution fusion | flops 4869586944 | bytes 36178944 | tf_op jit(solution)/shard_map/dot_general | solution.py:74
  331.3 7.9 %fusion.94 = (f32[3072]{0:T(1024)S(1)}, f32[3072,512]{1,0:T(8,128)S(1)}) fusion(bf16[3072,1536]{1,0:T(8,128)(2,1)} %bitcast.200, bf16[1,1536,512]{2,1,0:T(8,128)(2,1)S(1)} %copy-done.15), kind=kOutput, calls=%fused_computation.190 | convolution fusion | flops 4833408000 | bytes 17313792 | tf_op jit(solution)/shard_map/dot_general | solution.py:81
  339.2 2.1 multiply_reduce_fusion
  341.4 3.0 fusion
  344.4 3.3 reduce_sum.162
  347.7 5.1 %fusion.95 = (f32[512]{0:T(512)S(1)}, f32[512,512]{1,0:T(8,128)S(1)}) fusion(bf16[1,1536,512]{2,1,0:T(8,128)(2,1)} %param.43, f32[512,1536]{1,0:T(8,128)} %fusion.37, bf16[512,512]{1,0:T(8,128)(2,1)} %reduce_sum.162, bf16[1,512,1536]{2,1,0:T(8,128)(2,1)} %param.41, f32[1536]{0:T(1024)S(1)} %reduce.7), kind=kOutput, calls=%fused_computation.191 | convolution fusion | flops 1616379392 | bytes 7872512 | tf_op jit(solution)/shard_map/dot_general | solution.py:92
  (193 shorter events, 41.9 us)
Async XLA Ops:
  0.6 219.2 %copy-start = (bf16[1,512,1536]{2,1,0:T(8,128)(2,1)S(1)}, bf16[1,512,1536]{2,1,0:T(8,128)(2,1)}, u32[]{:S(2)}) copy-start(bf16[1,512,1536]{2,1,0:T(8,128)(2,1)} %param.33) | copy-start | bytes 4718596
  2.2 269.7 %collective-permute-start = (bf16[3,16,512]{2,1,0:T(8,128)(2,1)}, bf16[3,16,512]{2,1,0:T(8,128)(2,1)}, u32[]{:S(2)}, u32[]{:S(2)}) collective-permute-start(bf16[3,16,512]{2,1,0:T(8,128)(2,1)} %get-tuple-element.9), channel_id=1, source_target_pairs={{0,16},{16,32},{32,48},{48,64},{64,80},{80,96},{96,112},{112,0},{1... | collective-permute-start | bytes 147464 | tf_op jit(solution)/shard_map/ppermute | solution.py:21
  3.8 269.0 %collective-permute-start.1 = (bf16[3,16,512]{2,1,0:T(8,128)(2,1)}, bf16[3,16,512]{2,1,0:T(8,128)(2,1)}, u32[]{:S(2)}, u32[]{:S(2)}) collective-permute-start(bf16[3,16,512]{2,1,0:T(8,128)(2,1)} %get-tuple-element.8), channel_id=1, source_target_pairs={{16,0},{32,16},{48,32},{64,48},{80,64},{96,80},{112,96},{0,112},{1... | collective-permute-start | bytes 147464 | tf_op jit(solution)/shard_map/ppermute | solution.py:22
  7.1 4.8 %copy-start.23 = (bf16[8,4,512]{2,0,1:T(8,128)(2,1)}, bf16[8,4,512]{2,0,1:T(8,128)(2,1)S(1)}, u32[]{:S(2)}) copy-start(bf16[8,4,512]{2,0,1:T(8,128)(2,1)S(1)} %copy.115) | copy-start | bytes 98308
  7.8 235.6 %collective-permute-start.4 = (bf16[1,4,512]{2,0,1:T(2,128)(2,1)}, bf16[1,4,512]{2,0,1:T(2,128)(2,1)}, u32[]{:S(2)}, u32[]{:S(2)}) collective-permute-start(bf16[1,4,512]{2,0,1:T(2,128)(2,1)} %get-tuple-element.12), channel_id=1, source_target_pairs={{0,16},{16,32},{32,48},{48,64},{64,80},{80,96},{96,112},{112,0},{1... | collective-permute-start | bytes 12296 | tf_op jit(solution)/shard_map/ppermute | solution.py:21
  7.8 235.6 %collective-permute-start.5 = (bf16[1,4,512]{2,0,1:T(2,128)(2,1)}, bf16[1,4,512]{2,0,1:T(2,128)(2,1)}, u32[]{:S(2)}, u32[]{:S(2)}) collective-permute-start(bf16[1,4,512]{2,0,1:T(2,128)(2,1)} %get-tuple-element.13), channel_id=1, source_target_pairs={{16,0},{32,16},{48,32},{64,48},{80,64},{96,80},{112,96},{0,112},{1... | collective-permute-start | bytes 12296 | tf_op jit(solution)/shard_map/ppermute | solution.py:22
  20.0 179.4 %copy-start.41 = (f32[1,1536]{1,0:T(1,128)S(1)}, f32[1,1536]{1,0:T(1,128)}, u32[]{:S(2)}) copy-start(f32[1,1536]{1,0:T(1,128)} %param.36) | copy-start | bytes 18436
  20.0 179.4 %copy-start.1 = (bf16[1,512,1536]{2,1,0:T(8,128)(2,1)S(1)}, bf16[1,512,1536]{2,1,0:T(8,128)(2,1)}, u32[]{:S(2)}) copy-start(bf16[1,512,1536]{2,1,0:T(8,128)(2,1)} %param.40) | copy-start | bytes 4718596
  199.4 3.9 %copy-start.3 = (bf16[1,512,1536]{2,1,0:T(8,128)(2,1)S(1)}, bf16[1,512,1536]{2,1,0:T(8,128)(2,1)}, u32[]{:S(2)}) copy-start(bf16[1,512,1536]{2,1,0:T(8,128)(2,1)} %param.35) | copy-start | bytes 4718596
  199.4 3.9 %copy-start.6 = (bf16[32,16,512]{2,1,0:T(8,128)(2,1)S(1)}, bf16[32,16,512]{2,1,0:T(8,128)(2,1)}, u32[]{:S(2)}) copy-start(bf16[32,16,512]{2,1,0:T(8,128)(2,1)} %param.24) | copy-start | bytes 1572868
  207.7 3.3 copy-start.42
  219.9 7.3 %copy-start.13 = (bf16[1,1536,512]{2,1,0:T(8,128)(2,1)S(1)}, bf16[1,1536,512]{2,1,0:T(8,128)(2,1)}, u32[]{:S(2)}) copy-start(bf16[1,1536,512]{2,1,0:T(8,128)(2,1)} %param.37) | copy-start | bytes 4718596
  232.3 5.6 %copy-start.5 = (bf16[1536,512]{1,0:T(8,128)(2,1)}, bf16[1536,512]{1,0:T(8,128)(2,1)S(1)}, u32[]{:S(2)}) copy-start(bf16[1536,512]{1,0:T(8,128)(2,1)S(1)} %fusion.2) | copy-start | bytes 4718596
  233.5 6.3 %copy-start.35 = (f32[1,512]{1,0:T(1,128)S(1)}, f32[1,512]{1,0:T(1,128)}, u32[]{:S(2)}) copy-start(f32[1,512]{1,0:T(1,128)} %param.45) | copy-start | bytes 6148
  233.5 6.3 %copy-start.37 = (f32[1,512]{1,0:T(1,128)S(1)}, f32[1,512]{1,0:T(1,128)}, u32[]{:S(2)}) copy-start(f32[1,512]{1,0:T(1,128)} %param.44) | copy-start | bytes 6148
  237.9 3.2 copy-start.11
  241.1 9.5 %copy-start.20 = (bf16[6,8,4,512]{3,2,1,0:T(4,128)(2,1)S(1)}, bf16[6,8,4,512]{3,2,1,0:T(4,128)(2,1)}, u32[]{:S(2)}) copy-start(bf16[6,8,4,512]{3,2,1,0:T(4,128)(2,1)} %param.28) | copy-start | bytes 589828
  244.7 10.2 %collective-permute-start.6 = (bf16[10,1,512]{2,0,1:T(8,128)(2,1)}, bf16[10,1,512]{2,0,1:T(8,128)(2,1)}, u32[]{:S(2)}, u32[]{:S(2)}) collective-permute-start(bf16[10,1,512]{2,0,1:T(8,128)(2,1)} %get-tuple-element.10), channel_id=1, source_target_pairs={{0,1},{1,2},{2,3},{3,4},{4,5},{5,6},{6,7},{7,8},{8,9},{9,10},{10,1... | collective-permute-start | bytes 30728 | tf_op jit(solution)/shard_map/ppermute | solution.py:21
  244.8 10.1 %collective-permute-start.7 = (bf16[10,1,512]{2,0,1:T(8,128)(2,1)}, bf16[10,1,512]{2,0,1:T(8,128)(2,1)}, u32[]{:S(2)}, u32[]{:S(2)}) collective-permute-start(bf16[10,1,512]{2,0,1:T(8,128)(2,1)} %get-tuple-element.11), channel_id=1, source_target_pairs={{1,0},{2,1},{3,2},{4,3},{5,4},{6,5},{7,6},{8,7},{9,8},{10,9},{11,1... | collective-permute-start | bytes 30728 | tf_op jit(solution)/shard_map/ppermute | solution.py:22
  252.4 8.7 %copy-start.2 = (bf16[1,512,1536]{2,1,0:T(8,128)(2,1)S(1)}, bf16[1,512,1536]{2,1,0:T(8,128)(2,1)}, u32[]{:S(2)}) copy-start(bf16[1,512,1536]{2,1,0:T(8,128)(2,1)} %param.40) | copy-start | bytes 4718596
  261.1 3.8 %copy-start.39 = (s32[1024]{0:T(1024)S(1)}, s32[1024]{0:T(1024)}, u32[]{:S(2)}) copy-start(s32[1024]{0:T(1024)} %get-tuple-element.26) | copy-start | bytes 12292
  268.8 3.0 copy-start.22
  268.9 3.9 %copy-start.7 = (bf16[32,16,512]{2,1,0:T(8,128)(2,1)S(1)}, bf16[32,16,512]{2,1,0:T(8,128)(2,1)}, u32[]{:S(2)}) copy-start(bf16[32,16,512]{2,1,0:T(8,128)(2,1)} %param.24) | copy-start | bytes 1572868
  271.6 9.1 %copy-start.12 = (bf16[1,512,512]{2,1,0:T(8,128)(2,1)S(1)}, bf16[1,512,512]{2,1,0:T(8,128)(2,1)}, u32[]{:S(2)}) copy-start(bf16[1,512,512]{2,1,0:T(8,128)(2,1)} %param.46) | copy-start | bytes 1572868
  271.9 9.9 %copy-start.25 = (bf16[8,4,512]{2,1,0:T(4,128)(2,1)}, bf16[8,4,512]{2,1,0:T(4,128)(2,1)S(1)}, u32[]{:S(2)}) copy-start(bf16[8,4,512]{2,1,0:T(4,128)(2,1)S(1)} %reshape.539) | copy-start | bytes 98308
  275.3 8.5 %collective-permute-start.2 = (bf16[38,3,512]{2,1,0:T(4,128)(2,1)}, bf16[38,3,512]{2,1,0:T(4,128)(2,1)S(1)}, u32[]{:S(2)}, u32[]{:S(2)}) collective-permute-start(bf16[38,3,512]{2,1,0:T(4,128)(2,1)} %get-tuple-element.6), channel_id=1, source_target_pairs={{0,1},{1,2},{2,3},{3,4},{4,5},{5,6},{6,7},{7,8},{8,9},{9,10},{10,1... | collective-permute-start | bytes 350216 | tf_op jit(solution)/shard_map/ppermute | solution.py:21
  275.3 8.5 %collective-permute-start.3 = (bf16[38,3,512]{2,1,0:T(4,128)(2,1)}, bf16[38,3,512]{2,1,0:T(4,128)(2,1)S(1)}, u32[]{:S(2)}, u32[]{:S(2)}) collective-permute-start(bf16[38,3,512]{2,1,0:T(4,128)(2,1)} %get-tuple-element.7), channel_id=1, source_target_pairs={{1,0},{2,1},{3,2},{4,3},{5,4},{6,5},{7,6},{8,7},{9,8},{10,9},{11,1... | collective-permute-start | bytes 350216 | tf_op jit(solution)/shard_map/ppermute | solution.py:22
  283.2 5.3 %copy-start.4 = (bf16[1,512,1536]{2,1,0:T(8,128)(2,1)S(1)}, bf16[1,512,1536]{2,1,0:T(8,128)(2,1)}, u32[]{:S(2)}) copy-start(bf16[1,512,1536]{2,1,0:T(8,128)(2,1)} %param.34) | copy-start | bytes 4718596
  288.5 5.0 %copy-start.26 = (s32[3072]{0:T(1024)S(1)}, s32[3072]{0:T(1024)}, u32[]{:S(2)}) copy-start(s32[3072]{0:T(1024)} %broadcast_clamp_fusion) | copy-start | bytes 36868
  293.5 23.1 %copy-start.43 = (pred[6,512]{1,0:T(8,128)(4,1)S(1)}, pred[6,512]{1,0:T(8,128)(4,1)}, u32[]{:S(2)}) copy-start(pred[6,512]{1,0:T(8,128)(4,1)} %compare_and_fusion) | copy-start | bytes 9220
  316.6 14.7 %copy-start.15 = (bf16[1,1536,512]{2,1,0:T(8,128)(2,1)S(1)}, bf16[1,1536,512]{2,1,0:T(8,128)(2,1)}, u32[]{:S(2)}) copy-start(bf16[1,1536,512]{2,1,0:T(8,128)(2,1)} %param.37) | copy-start | bytes 4718596
  347.7 5.4 %copy-start.8 = (bf16[32,16,512]{2,1,0:T(8,128)(2,1)S(1)}, bf16[32,16,512]{2,1,0:T(8,128)(2,1)}, u32[]{:S(2)}) copy-start(bf16[32,16,512]{2,1,0:T(8,128)(2,1)} %param.24) | copy-start | bytes 1572868
  (21 other events, 36.3 us)
where the time goes:
time: 356 us; the launch traced here: 355 us
  blocking collectives  178 us (50%)
  matrix products  71 us (20%)
  local copies, waits for them, and re-layouts  57.6 us (16%)
  other arithmetic  27.2 us (8%)
  starting transfers between devices  19 us (5%)
    all_gather x2, blocking collectives, all_blocks(): blocks = lax.all_gather(blocks, axes[k], axis=0, tiled=True)  178 us
    gather x3, local copies, waits for them, and re-layouts, level_update(): jnp.take(sender_terms, senders.reshape(fanout, places), axis=0)  30.9 us
    dot_general x3, matrix products, level_update(): jnp.dot(flat_edges, self_matrix, preferred_element_type=jnp.float32)  23.7 us
    ppermute x4, starting transfers between devices, with_halo(): after = lax.ppermute(leading, axis, down)  17.2 us
    dot_general x3, matrix products, level_update(): jnp.dot(node_hidden, node_output, preferred_element_type=jnp.float32)  12.2 us
    dot_general x3, matrix products, level_update(): message = jnp.dot(hidden, edge_output, preferred_element_type=jnp.float32)  11.1 us
  transfers between devices with their start and end apart: 8, of which 1 were waited for; matrix products, arithmetic and copies ran while one was open for 22% of the time, Pallas kernels for 0%

commit v1 on v0

--- a/solution.py
+++ b/solution.py
@@ -33,7 +33,9 @@
 def all_blocks(value, axes, turns):
     blocks = value[None]
     for k in turns:
-        blocks = lax.all_gather(blocks, axes[k], axis=0, tiled=True)
+        blocks = jnp.concatenate(
+            lax.all_to_all(jnp.stack([blocks] * lax.axis_size(axes[k])), axes[k], 0, 0), axis=0
+        )
     block = [lax.axis_size(axes[k]) for k in reversed(turns)]
     blocks = blocks.reshape(*block, *value.shape)
     turned = sorted(range(len(turns)), key=lambda place: turns[len(turns) - 1 - place])

time: 356 us -> 187 us (0.53)
  blocking collectives: 178 us -> 4.08 us
  starting transfers between devices: 19 us -> 28.4 us
  local copies, waits for them, and re-layouts: 57.6 us -> 52.8 us
    all_gather x2 -> x0, blocking collectives: 178 us -> none  [all_blocks(): blocks = lax.all_gather(blocks, axes[k], axis=0, tiled=True)]
    all_to_all x0 -> x1, starting transfers between devices: none -> 9.42 us  [all_blocks(): lax.all_to_all(jnp.stack([blocks] * lax.axis_size(axes[k])), axes[k], 0, 0)]
    all_to_all x0 -> x1, blocking collectives: none -> 4.08 us  [all_blocks(): lax.all_to_all(jnp.stack([blocks] * lax.axis_size(axes[k])), axes[k], 0, 0)]
    reshape x6, local copies, waits for them, and re-layouts: 4.53 us -> 0.53 us  [level_update(): senders.reshape(fanout, places)]
  transfers between devices with their start and end apart: 8 -> 9, of which waited for: 1 -> 0; matrix products, arithmetic and copies ran while one was open for 22% -> 41% of each run, Pallas kernels for 0% -> 0%
where the time goes in v1:
time: 187 us; the launch traced here: 185 us
  matrix products  69.2 us (37%)
  local copies, waits for them, and re-layouts  52.8 us (28%)
  other arithmetic  29 us (16%)
  starting transfers between devices  28.4 us (15%)
  blocking collectives  4.08 us (2%)
    gather x3, local copies, waits for them, and re-layouts, level_update(): jnp.take(sender_terms, senders.reshape(fanout, places), axis=0)  31 us
    dot_general x3, matrix products, level_update(): jnp.dot(flat_edges, self_matrix, preferred_element_type=jnp.float32)  23.7 us
    ppermute x4, starting transfers between devices, with_halo(): after = lax.ppermute(leading, axis, down)  15.8 us
    dot_general x3, matrix products, level_update(): jnp.dot(node_hidden, node_output, preferred_element_type=jnp.float32)  12.2 us
    dot_general x3, matrix products, level_update(): message = jnp.dot(hidden, edge_output, preferred_element_type=jnp.float32)  11.4 us
    all_to_all x1, starting transfers between devices, all_blocks(): lax.all_to_all(jnp.stack([blocks] * lax.axis_size(axes[k])), axes[k], 0, 0)  9.42 us
    dot_general x3, matrix products, level_update(): jnp.dot(flat_nodes, receiver_matrix, preferred_element_type=jnp.float32)  6.83 us
    dot_general x3, matrix products, level_update(): jnp.dot(flat_nodes, node_self, preferred_element_type=jnp.float32)  6.03 us
  transfers between devices with their start and end apart: 9, of which 0 were waited for; matrix products, arithmetic and copies ran while one was open for 41% of the time, Pallas kernels for 0%

profile of v1, /device:TPU:0, one launch (start us, length us, event | category | flops | bytes accessed | tf_op | source)
XLA Modules:
  0.0 184.8 jit_solution(5254437568697045630)
XLA Ops:
  0.7 1.6 fusion.85
  2.3 1.6 collective-permute-start
  3.9 2.5 %collective-permute-start.1 = (bf16[3,16,512]{2,1,0:T(8,128)(2,1)}, bf16[3,16,512]{2,1,0:T(8,128)(2,1)}, u32[]{:S(2)}, u32[]{:S(2)}) collective-permute-start(bf16[3,16,512]{2,1,0:T(8,128)(2,1)} %get-tuple-element.8), channel_id=1, source_target_pairs={{16,0},{32,16},{48,32},{64,48},{80,64},{96,80},{112,96},{0,112},{1... | collective-permute-start | bytes 147464 | tf_op jit(solution)/shard_map/ppermute | solution.py:22
  10.0 9.4 %all-to-all-start = ((bf16[64,1,1,2,1,512]{5,3,4,2,1,0:T(2,128)(2,1)}), bf16[64,1,1,2,1,512]{5,3,4,2,1,0:T(2,128)(2,1)S(1)}, u32[]{:S(2)}, u32[]{:S(2)}) async-start(bf16[64,1,1,2,1,512]{5,3,4,2,1,0:T(2,128)(2,1)} %stack.6), calls=%async_computation | async-start | bytes 262144 | tf_op jit(solution)/shard_map/all_to_all | solution.py:37
  20.8 1.6 collective-permute-start.4
  22.3 2.6 %collective-permute-start.5 = (bf16[1,4,512]{2,0,1:T(2,128)(2,1)}, bf16[1,4,512]{2,0,1:T(2,128)(2,1)}, u32[]{:S(2)}, u32[]{:S(2)}) collective-permute-start(bf16[1,4,512]{2,0,1:T(2,128)(2,1)} %get-tuple-element.13), channel_id=1, source_target_pairs={{16,0},{32,16},{48,32},{64,48},{80,64},{96,80},{112,96},{0,112},{1... | collective-permute-start | bytes 12296 | tf_op jit(solution)/shard_map/ppermute | solution.py:22
  30.9 3.9 %fusion.37 = f32[512,1536]{1,0:T(8,128)} fusion(bf16[512,512]{1,0:T(8,128)(2,1)} %bitcast.179, bf16[1,512,1536]{2,1,0:T(8,128)(2,1)S(1)} %copy-done.1), kind=kOutput, calls=%fused_computation.56 | convolution fusion | flops 805306368 | bytes 5242880 | tf_op jit(solution)/shard_map/dot_general | solution.py:89
  34.9 2.6 %convolution_add_fusion.1 = f32[512,1536]{1,0:T(8,128)} fusion(bf16[512,512]{1,0:T(8,128)(2,1)S(1)} %bitcast.180, bf16[1,512,1536]{2,1,0:T(8,128)(2,1)S(1)} %copy-done.3, f32[1536]{0:T(1024)S(1)} %reduce.6), kind=kOutput, calls=%fused_computation.12 | convolution fusion | flops 806092800 | bytes 5249024 | tf_op jit(solution)/shard_map/dot_general | solution.py:75
  42.2 5.4 %collective-permute-start.7 = (bf16[10,1,512]{2,0,1:T(8,128)(2,1)}, bf16[10,1,512]{2,0,1:T(8,128)(2,1)}, u32[]{:S(2)}, u32[]{:S(2)}) collective-permute-start(bf16[10,1,512]{2,0,1:T(8,128)(2,1)} %get-tuple-element.11), channel_id=1, source_target_pairs={{1,0},{2,1},{3,2},{4,3},{5,4},{6,5},{7,6},{8,7},{9,8},{10,9},{11,1... | collective-permute-start | bytes 30728 | tf_op jit(solution)/shard_map/ppermute | solution.py:22
  51.9 5.4 %collective-permute-start.3 = (bf16[38,3,512]{2,1,0:T(4,128)(2,1)}, bf16[38,3,512]{2,1,0:T(4,128)(2,1)}, u32[]{:S(2)}, u32[]{:S(2)}) collective-permute-start(bf16[38,3,512]{2,1,0:T(4,128)(2,1)} %get-tuple-element.7), channel_id=1, source_target_pairs={{1,0},{2,1},{3,2},{4,3},{5,4},{6,5},{7,6},{8,7},{9,8},{10,9},{11,1... | collective-permute-start | bytes 350216 | tf_op jit(solution)/shard_map/ppermute | solution.py:22
  57.3 4.1 %all_to_all.10 = bf16[2,64,1,2,1,512]{5,1,4,3,2,0:T(8,128)(2,1)S(1)} all-to-all(bf16[2,64,1,2,1,512]{5,1,4,3,2,0:T(8,128)(2,1)S(1)} %pad_maximum_fusion.1), channel_id=1, replica_groups=mesh['dx_0'=2,'dx_1'=4,'dy_0'=2,'dy_1'=4,'dy_2'=2] {'dy_2'}, dimensions={0} | all-to-all | bytes 524288 | tf_op jit(solution)/shard_map/all_to_all | solution.py:37
  61.7 1.7 convolution_add_fusion.3
  63.4 1.7 fusion.35
  65.7 6.7 %gather_fusion.1 = f32[1536,1536]{1,0:T(8,128)} fusion(f32[256,1536]{1,0:T(8,128)S(1)} %fusion.26, s32[2048]{0:T(1024)S(1)} %pad_clamp_fusion), kind=kCustom, calls=%fused_computation.1 | custom fusion | bytes 18880512 | tf_op jit(solution)/shard_map/jit(_take)/gather | solution.py:80
  72.4 7.3 %multiply_convert_fusion.1 = bf16[6,256,1536]{2,1,0:T(8,128)(2,1)S(1)} fusion(f32[6,256,1536]{2,1,0:T(8,128)} %bitcast.173, bf16[6,256,512]{2,1,0:T(8,128)(2,1)} %bitcast.184, f32[256,1536]{1,0:T(8,128)} %convolution_add_fusion.3, pred[6,256]{1,0:T(8,128)(4,1)S(1)} %copy-done.30, bf16[1,512,1536]{2,1,0:T(8,128)(2,1)S(1)} %copy-done), kind=kOutput, calls=%fused_computation.6 | convolution fusion | flops 2434793472 | bytes 18875904 | tf_op jit(solution)/shard_map/dot_general | solution.py:76
  79.7 2.7 %fusion.87 = (f32[1536]{0:T(1024)S(1)}, f32[1536,512]{1,0:T(8,128)S(1)}) fusion(bf16[1536,1536]{1,0:T(8,128)(2,1)S(1)} %bitcast.205, bf16[1,1536,512]{2,1,0:T(8,128)(2,1)S(1)} %copy-done.14), kind=kOutput, calls=%fused_computation.189 | convolution fusion | flops 2416704000 | bytes 9443328 | tf_op jit(solution)/shard_map/dot_general | solution.py:83
  86.3 4.4 %fusion.88 = (f32[256]{0:T(256)S(1)}, f32[256,512]{1,0:T(8,128)}) fusion(bf16[1,1536,512]{2,1,0:T(8,128)(2,1)} %param.43, f32[256,1536]{1,0:T(8,128)} %fusion.35, bf16[256,512]{1,0:T(8,128)(2,1)} %reduce_sum.170, bf16[1,512,1536]{2,1,0:T(8,128)(2,1)} %param.41, f32[1536]{0:T(1024)S(1)} %reduce.7), kind=kOutput, calls=%fused_computation.190 | convolution fusion | flops 808189696 | bytes 5512192 | tf_op jit(solution)/shard_map/dot_general | solution.py:94
  95.9 1.8 gather_fusion.3
  98.8 2.5 %convolution_add_fusion.6 = f32[32,1536]{1,0:T(8,128)} fusion(bf16[32,512]{1,0:T(8,128)(2,1)S(1)} %reshape.533, bf16[1,512,1536]{2,1,0:T(8,128)(2,1)} %param.35, f32[1536]{0:T(1024)S(1)} %reduce.6), kind=kOutput, calls=%fused_computation.24 | convolution fusion | flops 50380800 | bytes 1808384 | tf_op jit(solution)/shard_map/dot_general | solution.py:75
  101.6 1.8 fusion.24
  104.5 1.7 multiply_convert_fusion.4
  107.4 2.7 %fusion.92 = (f32[32]{0:T(128)S(1)}, f32[32,512]{1,0:T(8,128)S(1)}) fusion(bf16[1,1536,512]{2,1,0:T(8,128)(2,1)} %param.43, f32[32,1536]{1,0:T(8,128)S(1)} %fusion.33, bf16[32,512]{1,0:T(8,128)(2,1)S(1)} %reduce_sum.175, bf16[1,512,1536]{2,1,0:T(8,128)(2,1)} %param.41, f32[1536]{0:T(1024)S(1)} %reduce.7), kind=kOutput, calls=%fused_computation.192 | convolution fusion | flops 101023712 | bytes 3446912 | tf_op jit(solution)/shard_map/dot_general | solution.py:94
  113.0 2.7 %pad_maximum_fusion = bf16[38,22,512]{2,1,0:T(8,128)(2,1)} fusion(bf16[38,3,512]{2,1,0:T(4,128)(2,1)} %collective-permute-done.3, bf16[38,16,512]{2,1,0:T(8,128)(2,1)} %copy-done.19, bf16[38,3,512]{2,1,0:T(4,128)(2,1)} %collective-permute-done.2), kind=kLoop, calls=%fused_computation.68 | loop fusion | flops 2568192 | bytes 1712128 | tf_op jit(solution)/shard_map/concatenate | solution.py:23
  115.8 2.1 %reshape.524 = bf16[836,512]{1,0:T(8,128)(2,1)} reshape(bf16[38,22,512]{2,1,0:T(8,128)(2,1)} %pad_maximum_fusion) | data formatting | bytes 1712128 | tf_op jit(solution)/shard_map/reshape | solution.py:190
  117.9 5.0 %fusion.28 = f32[836,1536]{1,0:T(8,128)} fusion(bf16[836,512]{1,0:T(8,128)(2,1)} %reshape.524, bf16[1,512,1536]{2,1,0:T(8,128)(2,1)S(1)} %copy-done.6), kind=kOutput, calls=%fused_computation.47 | convolution fusion | flops 1314914304 | bytes 7565312 | tf_op jit(solution)/shard_map/dot_general | solution.py:189
  122.9 23.2 %gather_fusion = f32[3072,1536]{1,0:T(8,128)} fusion(f32[836,1536]{1,0:T(8,128)} %fusion.28, s32[3072]{0:T(1024)S(1)} %broadcast_clamp_fusion), kind=kCustom, calls=%fused_computation | custom fusion | bytes 37761024 | tf_op jit(solution)/shard_map/jit(_take)/gather | solution.py:80
  146.1 14.7 %multiply_convert_fusion = bf16[6,512,1536]{2,1,0:T(8,128)(2,1)} fusion(f32[6,512,1536]{2,1,0:T(8,128)} %bitcast.170, f32[512,1536]{1,0:T(8,128)} %convolution_add_fusion.1, pred[6,512]{1,0:T(8,128)(4,1)S(1)} %copy-done.29, bf16[6,512,512]{2,1,0:T(8,128)(2,1)} %bitcast.181, bf16[1,512,1536]{2,1,0:T(8,128)(2,1)S(1)} %copy-done), kind=kOutput, calls=%fused_computation.5 | convolution fusion | flops 4869586944 | bytes 36178944 | tf_op jit(solution)/shard_map/dot_general | solution.py:76
  160.9 8.1 %fusion.95 = (f32[3072]{0:T(1024)S(1)}, f32[3072,512]{1,0:T(8,128)S(1)}) fusion(bf16[3072,1536]{1,0:T(8,128)(2,1)} %bitcast.204, bf16[1,1536,512]{2,1,0:T(8,128)(2,1)S(1)} %copy-done.16), kind=kOutput, calls=%fused_computation.193 | convolution fusion | flops 4833408000 | bytes 17313792 | tf_op jit(solution)/shard_map/dot_general | solution.py:83
  169.0 2.1 %multiply_reduce_fusion = f32[3072]{0:T(1024)S(1)} fusion(f32[3072,512]{1,0:T(8,128)S(1)} %get-tuple-element.23, f32[3072]{0:T(1024)S(1)} %broadcast_multiply_fusion), kind=kLoop, calls=%fused_computation.9 | loop fusion | flops 4715520 | bytes 6316032 | tf_op jit(solution)/shard_map/reduce_sum | solution.py:52
  171.2 3.0 %fusion = bf16[3072,512]{1,0:T(8,128)(2,1)} fusion(f32[3072,512]{1,0:T(8,128)S(1)} %get-tuple-element.23, bf16[6,32,16,512]{3,2,1,0:T(8,128)(2,1)S(1)} %copy-done.11, f32[512]{0:T(512)S(1)} %bitcast.194, f32[512]{0:T(512)S(1)} %bitcast.197, f32[3072]{0:T(1024)S(1)} %add_rsqrt_fusion, f32[3072]{0:T(1024)S(1)} %broadcast_multiply_fusion), kind=kLoop, calls=%fused_computation.8 | loop fusion | flops 11010048 | bytes 12611584 | tf_op jit(solution)/shard_map/convert_element_type | solution.py:84
  174.2 3.3 %reduce_sum.162 = bf16[512,512]{1,0:T(8,128)(2,1)} reduce(bf16[6,512,512]{2,1,0:T(8,128)(2,1)} %bitcast.171, bf16[]{:T(256)} %constant.214.clone.1), dimensions={0}, to_apply=%region_2.3 | reduce | flops 1310720 | bytes 3670018 | tf_op jit(solution)/shard_map/reduce_sum | solution.py:88
  177.5 5.1 %fusion.96 = (f32[512]{0:T(512)S(1)}, f32[512,512]{1,0:T(8,128)S(1)}) fusion(bf16[1,1536,512]{2,1,0:T(8,128)(2,1)} %param.43, f32[512,1536]{1,0:T(8,128)} %fusion.37, bf16[512,512]{1,0:T(8,128)(2,1)} %reduce_sum.162, bf16[1,512,1536]{2,1,0:T(8,128)(2,1)} %param.41, f32[1536]{0:T(1024)S(1)} %reduce.7), kind=kOutput, calls=%fused_computation.194 | convolution fusion | flops 1616379392 | bytes 7872512 | tf_op jit(solution)/shard_map/dot_general | solution.py:94
  (173 shorter events, 38.3 us)
Async XLA Ops:
  0.6 71.8 %copy-start = (bf16[1,512,1536]{2,1,0:T(8,128)(2,1)S(1)}, bf16[1,512,1536]{2,1,0:T(8,128)(2,1)}, u32[]{:S(2)}) copy-start(bf16[1,512,1536]{2,1,0:T(8,128)(2,1)} %param.33) | copy-start | bytes 4718596
  0.6 25.4 %copy-start.22 = (s32[6,16,16]{2,1,0:T(8,128)S(1)}, s32[6,16,16]{2,1,0:T(8,128)}, u32[]{:S(2)}) copy-start(s32[6,16,16]{2,1,0:T(8,128)} %param.32) | copy-start | bytes 18436
  0.7 26.7 %copy-start.28 = (s32[6,8,4]{1,2,0:T(4,128)S(1)}, s32[6,8,4]{1,2,0:T(4,128)}, u32[]{:S(2)}) copy-start(s32[6,8,4]{1,2,0:T(4,128)} %param.29) | copy-start | bytes 2308
  0.7 30.2 %copy-start.1 = (bf16[1,512,1536]{2,1,0:T(8,128)(2,1)S(1)}, bf16[1,512,1536]{2,1,0:T(8,128)(2,1)}, u32[]{:S(2)}) copy-start(bf16[1,512,1536]{2,1,0:T(8,128)(2,1)} %param.40) | copy-start | bytes 4718596
  2.3 45.2 %collective-permute-start = (bf16[3,16,512]{2,1,0:T(8,128)(2,1)}, bf16[3,16,512]{2,1,0:T(8,128)(2,1)}, u32[]{:S(2)}, u32[]{:S(2)}) collective-permute-start(bf16[3,16,512]{2,1,0:T(8,128)(2,1)} %get-tuple-element.9), channel_id=1, source_target_pairs={{0,16},{16,32},{32,48},{48,64},{64,80},{80,96},{96,112},{112,0},{1... | collective-permute-start | bytes 147464 | tf_op jit(solution)/shard_map/ppermute | solution.py:21
  3.9 45.5 %collective-permute-start.1 = (bf16[3,16,512]{2,1,0:T(8,128)(2,1)}, bf16[3,16,512]{2,1,0:T(8,128)(2,1)}, u32[]{:S(2)}, u32[]{:S(2)}) collective-permute-start(bf16[3,16,512]{2,1,0:T(8,128)(2,1)} %get-tuple-element.8), channel_id=1, source_target_pairs={{16,0},{32,16},{48,32},{64,48},{80,64},{96,80},{112,96},{0,112},{1... | collective-permute-start | bytes 147464 | tf_op jit(solution)/shard_map/ppermute | solution.py:22
  10.0 47.3 %all-to-all-start = ((bf16[64,1,1,2,1,512]{5,3,4,2,1,0:T(2,128)(2,1)}), bf16[64,1,1,2,1,512]{5,3,4,2,1,0:T(2,128)(2,1)S(1)}, u32[]{:S(2)}, u32[]{:S(2)}) async-start(bf16[64,1,1,2,1,512]{5,3,4,2,1,0:T(2,128)(2,1)} %stack.6), calls=%async_computation | async-start | bytes 262144 | tf_op jit(solution)/shard_map/all_to_all | solution.py:37
  20.8 20.1 %collective-permute-start.4 = (bf16[1,4,512]{2,0,1:T(2,128)(2,1)}, bf16[1,4,512]{2,0,1:T(2,128)(2,1)S(1)}, u32[]{:S(2)}, u32[]{:S(2)}) collective-permute-start(bf16[1,4,512]{2,0,1:T(2,128)(2,1)} %get-tuple-element.12), channel_id=1, source_target_pairs={{0,16},{16,32},{32,48},{48,64},{64,80},{80,96},{96,112},{112,0},{1... | collective-permute-start | bytes 12296 | tf_op jit(solution)/shard_map/ppermute | solution.py:21
  22.3 18.5 %collective-permute-start.5 = (bf16[1,4,512]{2,0,1:T(2,128)(2,1)}, bf16[1,4,512]{2,0,1:T(2,128)(2,1)}, u32[]{:S(2)}, u32[]{:S(2)}) collective-permute-start(bf16[1,4,512]{2,0,1:T(2,128)(2,1)} %get-tuple-element.13), channel_id=1, source_target_pairs={{16,0},{32,16},{48,32},{64,48},{80,64},{96,80},{112,96},{0,112},{1... | collective-permute-start | bytes 12296 | tf_op jit(solution)/shard_map/ppermute | solution.py:22
  30.9 3.9 %copy-start.3 = (bf16[1,512,1536]{2,1,0:T(8,128)(2,1)S(1)}, bf16[1,512,1536]{2,1,0:T(8,128)(2,1)}, u32[]{:S(2)}) copy-start(bf16[1,512,1536]{2,1,0:T(8,128)(2,1)} %param.35) | copy-start | bytes 4718596
  30.9 3.9 %copy-start.8 = (bf16[32,16,512]{2,1,0:T(8,128)(2,1)S(1)}, bf16[32,16,512]{2,1,0:T(8,128)(2,1)}, u32[]{:S(2)}) copy-start(bf16[32,16,512]{2,1,0:T(8,128)(2,1)} %param.24) | copy-start | bytes 1572868
  34.8 2.7 %copy-start.33 = (s32[10]{0:T(128)S(1)}, s32[10]{0:T(128)}, u32[]{:S(2)}) copy-start(s32[10]{0:T(128)} %fusion.78) | copy-start | bytes 124
  34.8 3.8 %copy-start.21 = (bf16[6,8,4,512]{3,2,1,0:T(4,128)(2,1)S(1)}, bf16[6,8,4,512]{3,2,1,0:T(4,128)(2,1)}, u32[]{:S(2)}) copy-start(bf16[6,8,4,512]{3,2,1,0:T(4,128)(2,1)} %param.28) | copy-start | bytes 589828
  42.2 55.6 %collective-permute-start.6 = (bf16[10,1,512]{2,0,1:T(8,128)(2,1)}, bf16[10,1,512]{2,0,1:T(8,128)(2,1)}, u32[]{:S(2)}, u32[]{:S(2)}) collective-permute-start(bf16[10,1,512]{2,0,1:T(8,128)(2,1)} %get-tuple-element.10), channel_id=1, source_target_pairs={{0,1},{1,2},{2,3},{3,4},{4,5},{5,6},{6,7},{7,8},{8,9},{9,10},{10,1... | collective-permute-start | bytes 30728 | tf_op jit(solution)/shard_map/ppermute | solution.py:21
  42.2 55.6 %collective-permute-start.7 = (bf16[10,1,512]{2,0,1:T(8,128)(2,1)}, bf16[10,1,512]{2,0,1:T(8,128)(2,1)}, u32[]{:S(2)}, u32[]{:S(2)}) collective-permute-start(bf16[10,1,512]{2,0,1:T(8,128)(2,1)} %get-tuple-element.11), channel_id=1, source_target_pairs={{1,0},{2,1},{3,2},{4,3},{5,4},{6,5},{7,6},{8,7},{9,8},{10,9},{11,1... | collective-permute-start | bytes 30728 | tf_op jit(solution)/shard_map/ppermute | solution.py:22
  51.9 61.2 %collective-permute-start.2 = (bf16[38,3,512]{2,1,0:T(4,128)(2,1)}, bf16[38,3,512]{2,1,0:T(4,128)(2,1)}, u32[]{:S(2)}, u32[]{:S(2)}) collective-permute-start(bf16[38,3,512]{2,1,0:T(4,128)(2,1)} %get-tuple-element.6), channel_id=1, source_target_pairs={{0,1},{1,2},{2,3},{3,4},{4,5},{5,6},{6,7},{7,8},{8,9},{9,10},{10,1... | collective-permute-start | bytes 350216 | tf_op jit(solution)/shard_map/ppermute | solution.py:21
  51.9 61.2 %collective-permute-start.3 = (bf16[38,3,512]{2,1,0:T(4,128)(2,1)}, bf16[38,3,512]{2,1,0:T(4,128)(2,1)}, u32[]{:S(2)}, u32[]{:S(2)}) collective-permute-start(bf16[38,3,512]{2,1,0:T(4,128)(2,1)} %get-tuple-element.7), channel_id=1, source_target_pairs={{1,0},{2,1},{3,2},{4,3},{5,4},{6,5},{7,6},{8,7},{9,8},{10,9},{11,1... | collective-permute-start | bytes 350216 | tf_op jit(solution)/shard_map/ppermute | solution.py:22
  57.2 4.4 %copy-start.4 = (bf16[1,512,1536]{2,1,0:T(8,128)(2,1)S(1)}, bf16[1,512,1536]{2,1,0:T(8,128)(2,1)}, u32[]{:S(2)}) copy-start(bf16[1,512,1536]{2,1,0:T(8,128)(2,1)} %param.35) | copy-start | bytes 4718596
  65.7 6.7 %copy-start.30 = (pred[6,256]{1,0:T(8,128)(4,1)S(1)}, pred[6,256]{1,0:T(8,128)(4,1)}, u32[]{:S(2)}) copy-start(pred[6,256]{1,0:T(8,128)(4,1)} %compare_and_fusion.1) | copy-start | bytes 4612
  72.4 7.3 %copy-start.14 = (bf16[1,1536,512]{2,1,0:T(8,128)(2,1)S(1)}, bf16[1,1536,512]{2,1,0:T(8,128)(2,1)}, u32[]{:S(2)}) copy-start(bf16[1,1536,512]{2,1,0:T(8,128)(2,1)} %param.37) | copy-start | bytes 4718596
  85.1 5.6 %copy-start.7 = (bf16[1536,512]{1,0:T(8,128)(2,1)}, bf16[1536,512]{1,0:T(8,128)(2,1)S(1)}, u32[]{:S(2)}) copy-start(bf16[1536,512]{1,0:T(8,128)(2,1)S(1)} %fusion.2) | copy-start | bytes 4718596
  86.3 5.7 %copy-start.26 = (f32[1,512]{1,0:T(1,128)S(1)}, f32[1,512]{1,0:T(1,128)}, u32[]{:S(2)}) copy-start(f32[1,512]{1,0:T(1,128)} %param.45) | copy-start | bytes 6148
  86.3 5.7 %copy-start.27 = (f32[1,512]{1,0:T(1,128)S(1)}, f32[1,512]{1,0:T(1,128)}, u32[]{:S(2)}) copy-start(f32[1,512]{1,0:T(1,128)} %param.44) | copy-start | bytes 6148
  90.7 2.6 %copy-start.12 = (bf16[1,512,512]{2,1,0:T(8,128)(2,1)S(1)}, bf16[1,512,512]{2,1,0:T(8,128)(2,1)}, u32[]{:S(2)}) copy-start(bf16[1,512,512]{2,1,0:T(8,128)(2,1)} %param.46) | copy-start | bytes 1572868
  92.0 2.8 %copy-start.34 = (pred[10]{0:T(512)(128)(4,1)S(1)}, pred[10]{0:T(512)(128)(4,1)}, u32[]{:S(2)}) copy-start(pred[10]{0:T(512)(128)(4,1)} %compare_and_fusion.3) | copy-start | bytes 34
  94.0 3.8 %copy-start.32 = (pred[6]{0:T(512)(128)(4,1)S(1)}, pred[6]{0:T(512)(128)(4,1)}, u32[]{:S(2)}) copy-start(pred[6]{0:T(512)(128)(4,1)} %compare_and_fusion.4) | copy-start | bytes 22
  95.9 5.3 %copy-start.2 = (bf16[1,512,1536]{2,1,0:T(8,128)(2,1)S(1)}, bf16[1,512,1536]{2,1,0:T(8,128)(2,1)}, u32[]{:S(2)}) copy-start(bf16[1,512,1536]{2,1,0:T(8,128)(2,1)} %param.40) | copy-start | bytes 4718596
  107.4 3.1 %copy-start.13 = (bf16[1,512,512]{2,1,0:T(8,128)(2,1)S(1)}, bf16[1,512,512]{2,1,0:T(8,128)(2,1)}, u32[]{:S(2)}) copy-start(bf16[1,512,512]{2,1,0:T(8,128)(2,1)} %param.46) | copy-start | bytes 1572868
  113.0 4.9 %copy-start.6 = (bf16[1,512,1536]{2,1,0:T(8,128)(2,1)S(1)}, bf16[1,512,1536]{2,1,0:T(8,128)(2,1)}, u32[]{:S(2)}) copy-start(bf16[1,512,1536]{2,1,0:T(8,128)(2,1)} %param.34) | copy-start | bytes 4718596
  122.9 23.2 %copy-start.29 = (pred[6,512]{1,0:T(8,128)(4,1)S(1)}, pred[6,512]{1,0:T(8,128)(4,1)}, u32[]{:S(2)}) copy-start(pred[6,512]{1,0:T(8,128)(4,1)} %compare_and_fusion) | copy-start | bytes 9220
  146.1 14.8 %copy-start.16 = (bf16[1,1536,512]{2,1,0:T(8,128)(2,1)S(1)}, bf16[1,1536,512]{2,1,0:T(8,128)(2,1)}, u32[]{:S(2)}) copy-start(bf16[1,1536,512]{2,1,0:T(8,128)(2,1)} %param.37) | copy-start | bytes 4718596
  177.5 5.4 %copy-start.9 = (bf16[32,16,512]{2,1,0:T(8,128)(2,1)S(1)}, bf16[32,16,512]{2,1,0:T(8,128)(2,1)}, u32[]{:S(2)}) copy-start(bf16[32,16,512]{2,1,0:T(8,128)(2,1)} %param.24) | copy-start | bytes 1572868
  (12 other events, 17.2 us)
